TPU v7x, 128 devices: a whole 4x4x4 slice. The times are simulated.
128 devices in a mesh: tm: 2 (over core), rows: 64 (over z, x, y).
Axes of the slice: x: 4, y: 4, z: 4, core: 2. Of those that a mesh axis runs over, the one named last changes fastest.
Arguments:
- feat: bfloat16 [4, 128, 240, 512], P('tm', 'rows'), may hold values from -24 to 24
- norm1_gain: float32 [512], replicated, may hold values from 0.5 to 1.5
- norm1_bias: float32 [512], replicated, may hold values from -3 to 3
- conv_weight: bfloat16 [3, 3, 3, 512, 512], replicated, may hold values from -0.0546875 to 0.0546875
- conv_bias: float32 [512], replicated, may hold values from -3 to 3
- norm2_gain: float32 [512], replicated, may hold values from 0.5 to 1.5
- norm2_bias: float32 [512], replicated, may hold values from -3 to 3
- w_query: bfloat16 [512, 512], replicated, may hold values from -0.44194174 to 0.44194174
- w_key: bfloat16 [512, 512], replicated, may hold values from -1.5467961 to 1.5467961
- w_value: bfloat16 [512, 512], replicated, may hold values from -0.25 to 0.25
- w_out: bfloat16 [512, 512], replicated, may hold values from -0.25 to 0.25
- out_bias: float32 [512], replicated, may hold values from -3 to 3
Outputs:
- block_out: bfloat16 [4, 128, 240, 512], P('tm', 'rows')
All inputs are finite; a program needn't handle non-finite values.
Results may differ from a plain program's by a relative error of at most 0.0062.
The roundings to bfloat16 on the way count: a program that leaves them out, or rounds other values in their place, can miss the bound.
Values may be sent and summed in bfloat16 or wider, within the bound.
No kernel may reach another device: no remote copies, remote signals or barrier semaphores. Data moves between devices by JAX's collectives and lax.ppermute only.
A program may use at most 128 MiB of HBM per device.

v0:
```python
import math
import jax
import jax.numpy as jnp
from jax import lax
from jax.sharding import PartitionSpec as P

GROUPS = 32
RADIUS = 4
EPS = 1e-06


def from_behind(array, axis, by):
    peers = lax.axis_size(axis)
    pairs = [(i, i + by) for i in range(peers) if 0 <= i + by < peers]
    return lax.ppermute(array, axis, pairs)


def padded_2(cells, sides, width):
    for axis, dim in sides:
        count = lax.axis_size(axis)
        ends = count - 1
        head = lax.slice_in_dim(cells, 0, width, axis=dim)
        tail = lax.slice_in_dim(cells, cells.shape[dim] - width, cells.shape[dim], axis=dim)
        cells = jnp.concatenate(
            [
                lax.ppermute(tail, axis, [(i, (i + 1) % count) for i in range(ends)]),
                cells,
                lax.ppermute(head, axis, [((i + 1) % count, i) for i in range(ends)]),
            ],
            axis=dim,
        )
    return cells


def group_norm(values, gain, shift, count):
    chans = values.shape[-1]
    grouped = values.reshape(values.shape[:-1] + (GROUPS, chans // GROUPS))
    local_sum = jnp.sum(grouped, axis=(0, 1, 2, 4))
    mean = lax.psum(local_sum, ("tm", "rows")) / count
    centered = grouped - mean[:, None]
    spread = lax.psum(jnp.sum(centered * centered, axis=(0, 1, 2, 4)), ("tm", "rows")) / count
    normed = centered * lax.rsqrt(spread + EPS)[:, None]
    return normed.reshape(values.shape) * gain + shift


def conv_taps(padded, weight, frames, height, width):
    chans = padded.shape[-1]
    total = jnp.zeros((frames * height * width, weight.shape[-1]), jnp.float32)
    for step_t in range(3):
        for step_h in range(3):
            slab = padded[step_t : step_t + frames, step_h : step_h + height]
            stacked = jnp.concatenate(
                [slab[:, :, step_w : step_w + width] for step_w in range(3)], axis=-1
            )
            total = total + jnp.dot(
                stacked.reshape(-1, 3 * chans),
                weight[step_t, step_h].reshape(3 * chans, -1),
                preferred_element_type=jnp.float32,
            )
    return total.reshape(frames, height, width, -1)


def project(flat, weight):
    return jnp.dot(flat, weight, preferred_element_type=jnp.float32).astype(jnp.bfloat16)


def shards(
    feat,
    norm1_gain,
    norm1_bias,
    conv_weight,
    conv_bias,
    norm2_gain,
    norm2_bias,
    w_query,
    w_key,
    w_value,
    w_out,
    out_bias,
):
    frames, stripe_rows, width, chans = feat.shape
    stripes = lax.axis_size("rows")
    count = lax.axis_size("tm") * stripes * frames * stripe_rows * width * (chans // GROUPS)
    act = jax.nn.silu(group_norm(feat.astype(jnp.float32), norm1_gain, norm1_bias, count)).astype(
        jnp.bfloat16
    )
    earlier = from_behind(act, "tm", 1)
    opening = jnp.broadcast_to(act[:1], earlier.shape)
    earlier = jnp.where(lax.axis_index("tm") == 0, opening, earlier)
    timed = jnp.concatenate([earlier, act], axis=0)
    rimmed = padded_2(timed, (("rows", 1),), 1)
    padded = jnp.pad(rimmed, ((0, 0), (0, 0), (1, 1), (0, 0)))
    conv = conv_taps(padded, conv_weight, frames, stripe_rows, width) + conv_bias
    resid = (feat.astype(jnp.float32) + conv).astype(jnp.bfloat16)
    normed = group_norm(resid.astype(jnp.float32), norm2_gain, norm2_bias, count).astype(
        jnp.bfloat16
    )
    flat = normed.reshape(-1, chans)
    query = project(flat, w_query).reshape(frames, -1, chans)
    reach = RADIUS * stripe_rows
    paired = jnp.stack([project(flat, w_key), project(flat, w_value)]).reshape(
        2, frames, stripe_rows, width, chans
    )
    pieces = []
    for offset in range(-RADIUS, RADIUS + 1):
        if offset == 0:
            pieces.append(paired)
        else:
            pieces.append(from_behind(paired, "rows", -offset))
    wide = jnp.concatenate(pieces, axis=2)
    keys = wide[0].reshape(frames, -1, chans)
    values = wide[1].reshape(frames, -1, chans)
    span = 2 * reach + stripe_rows
    place = lax.axis_index("rows") * stripe_rows - reach + jnp.arange(span, dtype=jnp.int32)
    valid = jnp.repeat((place >= 0) & (place < stripes * stripe_rows), width)
    scale = 1.0 / math.sqrt(chans)
    scores = jnp.einsum("fqc,fkc->fqk", query, keys, preferred_element_type=jnp.float32) * scale
    scores = jnp.where(valid[None, None, :], scores, jnp.float32(-1e30))
    top = jnp.max(scores, axis=-1, keepdims=True)
    expo = jnp.exp(scores - top)
    total = jnp.sum(expo, axis=-1, keepdims=True)
    mixed = jnp.einsum(
        "fqk,fkc->fqc", expo.astype(jnp.bfloat16), values, preferred_element_type=jnp.float32
    )
    attn = (mixed / total).astype(jnp.bfloat16).reshape(-1, chans)
    output = jnp.dot(attn, w_out, preferred_element_type=jnp.float32).reshape(
        frames, stripe_rows, width, chans
    )
    return (resid.astype(jnp.float32) + out_bias + output).astype(jnp.bfloat16)


def solution(mesh):
    return jax.shard_map(
        shards,
        mesh=mesh,
        in_specs=(
            P("tm", "rows", None, None),
            P(),
            P(),
            P(),
            P(),
            P(),
            P(),
            P(),
            P(),
            P(),
            P(),
            P(),
        ),
        out_specs=P("tm", "rows", None, None),
        check_vma=False,
    )
```

profile of v0, /device:TPU:54, one launch (start us, length us, event | category | flops | bytes accessed | tf_op | source)
XLA Modules:
  0.0 680.6 jit_solution(8682278299150185639)
XLA Ops:
  1.7 63.7 %psum.28 = f32[32]{0:T(128)S(1)} all-reduce(f32[32]{0:T(128)S(1)} %reduce_sum.59), channel_id=1, replica_groups=mesh['tm'=2,'rows'=64] {'tm','rows'}, use_global_device_ids=true, to_apply=%region_2.0 | all-reduce | flops 32 | bytes 256 | tf_op jit(solution)/shard_map/psum | solution.py:39
  67.2 63.0 %psum.29 = f32[32]{0:T(128)S(1)} all-reduce(f32[32]{0:T(128)S(1)} %reduce_sum.62), channel_id=1, replica_groups=mesh['tm'=2,'rows'=64] {'tm','rows'}, use_global_device_ids=true, to_apply=%region_5.6 | all-reduce | flops 32 | bytes 256 | tf_op jit(solution)/shard_map/psum | solution.py:41
  130.4 1.9 fusion.31
  132.3 1.7 collective-permute-start
  134.1 2.1 collective-permute-done
  136.5 3.7 collective-permute-start.1
  140.2 2.4 collective-permute-start.2
  142.5 9.3 %fusion.44 = (bf16[1,1,3,512,512]{4,3,2,1,0:T(8,128)(2,1)S(1)}, bf16[1,1,3,512,512]{4,3,2,1,0:T(8,128)(2,1)}, bf16[1,1,3,512,512]{4,3,2,1,0:T(8,128)(2,1)}, bf16...) fusion(bf16[3,3,3,512,512]{4,3,2,1,0:T(8,128)(2,1)} %param.15), kind=kLoop, calls=%fused_computation.89 | loop fusion | bytes 28311552 | tf_op jit(solution)/shard_map/slice | solution.py:57
  151.8 10.6 %collective-permute-done.1 = bf16[4,1,240,512]{3,2,1,0:T(8,128)(2,1)S(1)} collective-permute-done((bf16[4,1,240,512]{3,2,1,0:T(8,128)(2,1)S(1)}, bf16[4,1,240,512]{3,2,1,0:T(8,128)(2,1)S(1)}, u32[]{:S(2)}, u32[]{:S(2)}) %collective-permute-start.1) | collective-permute-done | bytes 983072 | tf_op jit(solution)/shard_map/ppermute | solution.py:26
  162.4 4.4 collective-permute-done.2
  166.8 2.1 select_maximum_fusion
  168.8 6.3 fusion.45
  179.5 1.7 fusion.48
  181.2 1.7 fusion.50
  184.7 1.7 fusion.51
  186.4 1.7 fusion.53
  189.5 1.7 fusion.54
  192.6 1.7 fusion.49
  194.3 1.7 fusion.52
  196.0 1.7 fusion.55
  197.7 2.5 add_add_fusion
  200.8 66.5 %psum.30 = f32[32]{0:T(128)S(1)} all-reduce(f32[32]{0:T(128)S(1)} %reduce_sum.81), channel_id=1, replica_groups=mesh['tm'=2,'rows'=64] {'tm','rows'}, use_global_device_ids=true, to_apply=%region_8.9 | all-reduce | flops 32 | bytes 256 | tf_op jit(solution)/shard_map/psum | solution.py:39
  268.0 64.1 %psum.31 = f32[32]{0:T(128)S(1)} all-reduce(f32[32]{0:T(128)S(1)} %reduce_sum.84), channel_id=1, replica_groups=mesh['tm'=2,'rows'=64] {'tm','rows'}, use_global_device_ids=true, to_apply=%region_11.12 | all-reduce | flops 32 | bytes 256 | tf_op jit(solution)/shard_map/psum | solution.py:41
  333.4 1.7 convolution_convert_fusion
  336.6 3.8 collective-permute-start.3
  340.4 3.2 collective-permute-start.4
  343.6 4.6 collective-permute-start.5
  348.2 3.0 collective-permute-start.6
  351.2 2.8 collective-permute-start.7
  354.1 30.5 %collective-permute-done.3 = bf16[2,2,2,240,512]{4,3,2,1,0:T(8,128)(2,1)} collective-permute-done((bf16[2,2,2,240,512]{4,3,2,1,0:T(8,128)(2,1)}, bf16[2,2,2,240,512]{4,3,2,1,0:T(8,128)(2,1)}, u32[]{:S(2)}, u32[]{:S(2)}) %collective-permute-start.3) | collective-permute-done | bytes 1966112 | tf_op jit(solution)/shard_map/ppermute | solution.py:15
  384.6 2.5 collective-permute-start.8
  387.1 39.4 %collective-permute-done.4 = bf16[2,2,2,240,512]{4,3,2,1,0:T(8,128)(2,1)} collective-permute-done((bf16[2,2,2,240,512]{4,3,2,1,0:T(8,128)(2,1)}, bf16[2,2,2,240,512]{4,3,2,1,0:T(8,128)(2,1)}, u32[]{:S(2)}, u32[]{:S(2)}) %collective-permute-start.4) | collective-permute-done | bytes 1966112 | tf_op jit(solution)/shard_map/ppermute | solution.py:15
  426.5 90.0 %collective-permute-start.9 = (bf16[2,2,2,240,512]{4,3,2,1,0:T(8,128)(2,1)}, bf16[2,2,2,240,512]{4,3,2,1,0:T(8,128)(2,1)}, u32[]{:S(2)}, u32[]{:S(2)}) collective-permute-start(bf16[2,2,2,240,512]{4,3,2,1,0:T(8,128)(2,1)} %pad_maximum_fusion.10), channel_id=1, source_target_pairs={{3,0},{4,1},{5,2},{6,3},{7,4},{8,5},{9,6},{10,7},{11,8},{12,9},{13... | collective-permute-start | bytes 5898248 | tf_op jit(solution)/shard_map/ppermute | solution.py:15
  516.5 3.1 collective-permute-start.10
  519.8 2.7 convolution_convert_fusion.2
  522.5 1.7 constant_dynamic-update-slice_fusion.8
  524.2 1.7 constant_dynamic-update-slice_fusion.7
  525.9 1.7 constant_dynamic-update-slice_fusion.6
  527.6 1.7 constant_dynamic-update-slice_fusion.5
  529.4 1.7 constant_dynamic-update-slice_fusion.3
  531.1 1.7 constant_dynamic-update-slice_fusion.2
  532.8 27.3 %collective-permute-done.9 = bf16[2,2,2,240,512]{4,3,2,1,0:T(8,128)(2,1)} collective-permute-done((bf16[2,2,2,240,512]{4,3,2,1,0:T(8,128)(2,1)}, bf16[2,2,2,240,512]{4,3,2,1,0:T(8,128)(2,1)}, u32[]{:S(2)}, u32[]{:S(2)}) %collective-permute-start.9) | collective-permute-done | bytes 1966112 | tf_op jit(solution)/shard_map/ppermute | solution.py:15
  561.7 80.5 %collective-permute-done.10 = bf16[2,2,2,240,512]{4,3,2,1,0:T(8,128)(2,1)} collective-permute-done((bf16[2,2,2,240,512]{4,3,2,1,0:T(8,128)(2,1)}, bf16[2,2,2,240,512]{4,3,2,1,0:T(8,128)(2,1)}, u32[]{:S(2)}, u32[]{:S(2)}) %collective-permute-start.10) | collective-permute-done | bytes 1966112 | tf_op jit(solution)/shard_map/ppermute | solution.py:15
  642.2 1.7 constant_dynamic-update-slice_fusion
  643.9 4.3 fusion.43
  648.2 10.2 %fusion = (f32[2,480]{1,0:T(2,128)S(1)}, f32[2,480,4320]{2,1,0:T(8,128)}) fusion(pred[4320]{0:T(1024)(128)(4,1)S(1)} %broadcast_in_dim.35, bf16[2,480,512]{2,1,0:T(8,128)(2,1)} %bitcast.89, bf16[2,4320,512]{2,1,0:T(8,128)(2,1)S(1)} %bitcast.63), kind=kOutput, calls=%fused_computation.2 | convolution fusion | flops 4259173376 | bytes 26427360 | tf_op jit(solution)/shard_map/fqc,fkc->fqk/dot_general | solution.py:117
  658.4 9.5 %fusion.1 = f32[2,480]{1,0:T(2,128)S(1)} fusion(f32[2,480,4320]{2,1,0:T(8,128)} %get-tuple-element.50, f32[2,480]{1,0:T(2,128)S(1)} %get-tuple-element.49, pred[4320]{0:T(1024)(128)(4,1)S(1)} %broadcast_in_dim.35), kind=kLoop, calls=%fused_computation.3 | loop fusion | flops 16587840 | bytes 16600800 | tf_op jit(solution)/shard_map/reduce_sum | solution.py:121
  667.9 11.0 %divide_convert_fusion = bf16[2,480,512]{2,1,0:T(8,128)(2,1)S(1)} fusion(bf16[2,4320,512]{2,1,0:T(8,128)(2,1)} %bitcast.62, f32[2,480,4320]{2,1,0:T(8,128)} %get-tuple-element.50, f32[2,480]{1,0:T(2,128)S(1)} %get-tuple-element.49, pred[4320]{0:T(1024)(128)(4,1)S(1)} %broadcast_in_dim.35, f32[2,480]{1,0:T(2,128)S(1)} %fusion.1), kind=kOutput, calls=%fused_computation.62 | convolution fusion | flops 4264304640 | bytes 26431200 | tf_op jit(solution)/shard_map/fqk,fkc->fqc/dot_general | solution.py:122
  (105 shorter events, 20.6 us)
Async XLA Ops:
  0.0 332.7 %copy-start = (bf16[512,512]{1,0:T(8,128)(2,1)S(1)}, bf16[512,512]{1,0:T(8,128)(2,1)}, u32[]{:S(2)}) copy-start(bf16[512,512]{1,0:T(8,128)(2,1)} %param.20) | copy-start | bytes 1572868
  132.3 3.9 collective-permute-start
  136.5 25.9 %collective-permute-start.1 = (bf16[4,1,240,512]{3,2,1,0:T(8,128)(2,1)S(1)}, bf16[4,1,240,512]{3,2,1,0:T(8,128)(2,1)S(1)}, u32[]{:S(2)}, u32[]{:S(2)}) collective-permute-start(bf16[4,1,240,512]{3,2,1,0:T(8,128)(2,1)S(1)} %get-tuple-element.44), channel_id=1, source_target_pairs={{0,1},{1,2},{2,3},{3,4},{4,5},{5,6},{6,7},{7,8},{8,9},{9,10},{10,1... | collective-permute-start | bytes 2949128 | tf_op jit(solution)/shard_map/ppermute | solution.py:26
  140.2 26.6 %collective-permute-start.2 = (bf16[4,1,240,512]{3,2,1,0:T(8,128)(2,1)S(1)}, bf16[4,1,240,512]{3,2,1,0:T(8,128)(2,1)S(1)}, u32[]{:S(2)}, u32[]{:S(2)}) collective-permute-start(bf16[4,1,240,512]{3,2,1,0:T(8,128)(2,1)S(1)} %get-tuple-element.45), channel_id=1, source_target_pairs={{1,0},{2,1},{3,2},{4,3},{5,4},{6,5},{7,6},{8,7},{9,8},{10,9},{11,1... | collective-permute-start | bytes 2949128 | tf_op jit(solution)/shard_map/ppermute | solution.py:28
  176.0 1.2 copy-start.10
  176.0 1.5 copy-start.11
  176.0 1.8 copy-start.12
  176.0 2.1 copy-start.13
  178.1 1.4 copy-start.21
  179.5 1.7 copy-start.20
  181.2 1.7 copy-start.6
  181.2 1.7 copy-start.7
  181.2 1.8 copy-start.8
  181.2 2.1 copy-start.9
  183.3 1.4 copy-start.19
  184.7 1.7 copy-start.18
  186.4 1.7 copy-start.5
  188.1 1.4 copy-start.17
  191.2 1.4 copy-start.16
  192.6 1.7 copy-start.15
  194.3 1.7 copy-start.14
  197.7 2.5 copy-start.2
  197.7 2.5 copy-start.24
  200.2 132.1 %copy-start.25 = (f32[512]{0:T(512)S(1)}, f32[512]{0:T(512)}, u32[]{:S(2)}) copy-start(f32[512]{0:T(512)} %param.18) | copy-start | bytes 6148
  200.2 132.1 %copy-start.26 = (f32[512]{0:T(512)S(1)}, f32[512]{0:T(512)}, u32[]{:S(2)}) copy-start(f32[512]{0:T(512)} %param.17) | copy-start | bytes 6148
  200.6 132.8 %copy-start.3 = (bf16[2,2,240,512]{3,2,1,0:T(8,128)(2,1)}, bf16[2,2,240,512]{3,2,1,0:T(8,128)(2,1)S(1)}, u32[]{:S(2)}) copy-start(bf16[2,2,240,512]{3,2,1,0:T(8,128)(2,1)S(1)} %get-tuple-element.6) | copy-start | bytes 2949124
  332.7 2.4 copy-start.22
  335.1 184.7 %copy-start.23 = (bf16[2,2,240,512]{3,2,1,0:T(8,128)(2,1)S(1)}, bf16[2,2,240,512]{3,2,1,0:T(8,128)(2,1)}, u32[]{:S(2)}) copy-start(bf16[2,2,240,512]{3,2,1,0:T(8,128)(2,1)} %copy-done.22) | copy-start | bytes 2949124
  336.6 48.0 %collective-permute-start.3 = (bf16[2,2,2,240,512]{4,3,2,1,0:T(8,128)(2,1)}, bf16[2,2,2,240,512]{4,3,2,1,0:T(8,128)(2,1)}, u32[]{:S(2)}, u32[]{:S(2)}) collective-permute-start(bf16[2,2,2,240,512]{4,3,2,1,0:T(8,128)(2,1)} %pad_maximum_fusion.10), channel_id=1, source_target_pairs={{0,4},{1,5},{2,6},{3,7},{4,8},{5,9},{6,10},{7,11},{8,12},{9,13},{1... | collective-permute-start | bytes 5898248 | tf_op jit(solution)/shard_map/ppermute | solution.py:15
  340.4 86.0 %collective-permute-start.4 = (bf16[2,2,2,240,512]{4,3,2,1,0:T(8,128)(2,1)}, bf16[2,2,2,240,512]{4,3,2,1,0:T(8,128)(2,1)}, u32[]{:S(2)}, u32[]{:S(2)}) collective-permute-start(bf16[2,2,2,240,512]{4,3,2,1,0:T(8,128)(2,1)} %pad_maximum_fusion.10), channel_id=1, source_target_pairs={{0,3},{1,4},{2,5},{3,6},{4,7},{5,8},{6,9},{7,10},{8,11},{9,12},{10... | collective-permute-start | bytes 5898248 | tf_op jit(solution)/shard_map/ppermute | solution.py:15
  343.6 172.8 %collective-permute-start.5 = (bf16[2,2,2,240,512]{4,3,2,1,0:T(8,128)(2,1)}, bf16[2,2,2,240,512]{4,3,2,1,0:T(8,128)(2,1)}, u32[]{:S(2)}, u32[]{:S(2)}) collective-permute-start(bf16[2,2,2,240,512]{4,3,2,1,0:T(8,128)(2,1)} %pad_maximum_fusion.10), channel_id=1, source_target_pairs={{0,2},{1,3},{2,4},{3,5},{4,6},{5,7},{6,8},{7,9},{8,10},{9,11},{10,... | collective-permute-start | bytes 5898248 | tf_op jit(solution)/shard_map/ppermute | solution.py:15
  348.2 179.4 %collective-permute-start.6 = (bf16[2,2,2,240,512]{4,3,2,1,0:T(8,128)(2,1)}, bf16[2,2,2,240,512]{4,3,2,1,0:T(8,128)(2,1)}, u32[]{:S(2)}, u32[]{:S(2)}) collective-permute-start(bf16[2,2,2,240,512]{4,3,2,1,0:T(8,128)(2,1)} %pad_maximum_fusion.10), channel_id=1, source_target_pairs={{0,1},{1,2},{2,3},{3,4},{4,5},{5,6},{6,7},{7,8},{8,9},{9,10},{10,1... | collective-permute-start | bytes 5898248 | tf_op jit(solution)/shard_map/ppermute | solution.py:15
  351.2 178.2 %collective-permute-start.7 = (bf16[2,2,2,240,512]{4,3,2,1,0:T(8,128)(2,1)}, bf16[2,2,2,240,512]{4,3,2,1,0:T(8,128)(2,1)}, u32[]{:S(2)}, u32[]{:S(2)}) collective-permute-start(bf16[2,2,2,240,512]{4,3,2,1,0:T(8,128)(2,1)} %pad_maximum_fusion.10), channel_id=1, source_target_pairs={{1,0},{2,1},{3,2},{4,3},{5,4},{6,5},{7,6},{8,7},{9,8},{10,9},{11,1... | collective-permute-start | bytes 5898248 | tf_op jit(solution)/shard_map/ppermute | solution.py:15
  384.6 146.5 %collective-permute-start.8 = (bf16[2,2,2,240,512]{4,3,2,1,0:T(8,128)(2,1)}, bf16[2,2,2,240,512]{4,3,2,1,0:T(8,128)(2,1)}, u32[]{:S(2)}, u32[]{:S(2)}) collective-permute-start(bf16[2,2,2,240,512]{4,3,2,1,0:T(8,128)(2,1)} %pad_maximum_fusion.10), channel_id=1, source_target_pairs={{2,0},{3,1},{4,2},{5,3},{6,4},{7,5},{8,6},{9,7},{10,8},{11,9},{12,... | collective-permute-start | bytes 5898248 | tf_op jit(solution)/shard_map/ppermute | solution.py:15
  426.5 133.6 %collective-permute-start.9 = (bf16[2,2,2,240,512]{4,3,2,1,0:T(8,128)(2,1)}, bf16[2,2,2,240,512]{4,3,2,1,0:T(8,128)(2,1)}, u32[]{:S(2)}, u32[]{:S(2)}) collective-permute-start(bf16[2,2,2,240,512]{4,3,2,1,0:T(8,128)(2,1)} %pad_maximum_fusion.10), channel_id=1, source_target_pairs={{3,0},{4,1},{5,2},{6,3},{7,4},{8,5},{9,6},{10,7},{11,8},{12,9},{13... | collective-permute-start | bytes 5898248 | tf_op jit(solution)/shard_map/ppermute | solution.py:15
  516.5 125.7 %collective-permute-start.10 = (bf16[2,2,2,240,512]{4,3,2,1,0:T(8,128)(2,1)}, bf16[2,2,2,240,512]{4,3,2,1,0:T(8,128)(2,1)}, u32[]{:S(2)}, u32[]{:S(2)}) collective-permute-start(bf16[2,2,2,240,512]{4,3,2,1,0:T(8,128)(2,1)} %pad_maximum_fusion.10), channel_id=1, source_target_pairs={{4,0},{5,1},{6,2},{7,3},{8,4},{9,5},{10,6},{11,7},{12,8},{13,9},{1... | collective-permute-start | bytes 5898248 | tf_op jit(solution)/shard_map/ppermute | solution.py:15
  667.9 11.1 %copy-start.4 = (bf16[2,2,240,512]{3,2,1,0:T(8,128)(2,1)S(1)}, bf16[2,2,240,512]{3,2,1,0:T(8,128)(2,1)}, u32[]{:S(2)}) copy-start(bf16[2,2,240,512]{3,2,1,0:T(8,128)(2,1)} %copy-done.3) | copy-start | bytes 2949124
  667.9 11.1 %copy-start.27 = (bf16[512,512]{1,0:T(8,128)(2,1)S(1)}, bf16[512,512]{1,0:T(8,128)(2,1)}, u32[]{:S(2)}) copy-start(bf16[512,512]{1,0:T(8,128)(2,1)} %param.22) | copy-start | bytes 1572868
  667.9 11.1 %copy-start.28 = (f32[512]{0:T(512)S(1)}, f32[512]{0:T(512)}, u32[]{:S(2)}) copy-start(f32[512]{0:T(512)} %param.23) | copy-start | bytes 6148
  667.9 12.7 %copy-start.1 = (bf16[512,512]{1,0:T(8,128)(2,1)S(1)}, bf16[512,512]{1,0:T(8,128)(2,1)}, u32[]{:S(2)}) copy-start(bf16[512,512]{1,0:T(8,128)(2,1)} %param.20) | copy-start | bytes 1572868
where the time goes:
time: 682 us; the launch traced here: 681 us
  blocking collectives  257 us (38%)
  waiting for transfers between devices  195 us (29%)
  starting transfers between devices  121 us (18%)
  matrix products  43.8 us (6%)
  local copies, waits for them, and re-layouts  40.4 us (6%)
  other arithmetic  22.8 us (3%)
    ppermute x9, waiting for transfers between devices, from_behind(): return lax.ppermute(array, axis, pairs)  180 us
    psum x2, blocking collectives, group_norm(): mean = lax.psum(local_sum, ('tm', 'rows')) / count  130 us
    psum x2, blocking collectives, group_norm(): lax.psum(jnp.sum(centered * centered, axis=(0, 1, 2, 4)), ('tm', 'rows'))  127 us
    ppermute x9, starting transfers between devices, from_behind(): return lax.ppermute(array, axis, pairs)  115 us
    unnamed x65, local copies, waits for them, and re-layouts  17.3 us
    dot_general x9, matrix products, conv_taps(): jnp.dot(stacked.reshape(-1, 3 * chans), weight[step_t, step_h].reshape(3...  15.9 us
  transfers between devices with their start and end apart: 11, of which 7 were waited for; matrix products, arithmetic and copies ran while one was open for 4% of the time, Pallas kernels for 0%

commit v1 on v0

--- a/solution.py
+++ b/solution.py
@@ -3,6 +3,7 @@
 import jax.numpy as jnp
 from jax import lax
 from jax.sharding import PartitionSpec as P
+from jax.lax import all_gather
 
 GROUPS = 32
 RADIUS = 4
@@ -38,7 +39,13 @@
     local_sum = jnp.sum(grouped, axis=(0, 1, 2, 4))
     mean = lax.psum(local_sum, ("tm", "rows")) / count
     centered = grouped - mean[:, None]
-    spread = lax.psum(jnp.sum(centered * centered, axis=(0, 1, 2, 4)), ("tm", "rows")) / count
+    spread = (
+        jnp.sum(
+            all_gather(jnp.sum(centered * centered, axis=(0, 1, 2, 4)), axis_name=("tm", "rows")),
+            axis=0,
+        )
+        / count
+    )
     normed = centered * lax.rsqrt(spread + EPS)[:, None]
     return normed.reshape(values.shape) * gain + shift
 

time: 682 us -> 683 us (level)
    unnamed x0 -> x2, blocking collectives: none -> 127 us
    psum x2 -> x0, blocking collectives: 127 us -> none  [group_norm(): lax.psum(jnp.sum(centered * centered, axis=(0, 1, 2, 4)), ('tm', 'rows'))]
    unnamed x65 -> x71, local copies, waits for them, and re-layouts: 17.3 us -> 17.4 us
where the time goes in v1:
time: 683 us; the launch traced here: 682 us
  blocking collectives  257 us (38%)
  waiting for transfers between devices  195 us (29%)
  starting transfers between devices  121 us (18%)
  matrix products  46.7 us (7%)
  local copies, waits for them, and re-layouts  38.9 us (6%)
  other arithmetic  22.4 us (3%)
    ppermute x9, waiting for transfers between devices, from_behind(): return lax.ppermute(array, axis, pairs)  180 us
    psum x2, blocking collectives, group_norm(): mean = lax.psum(local_sum, ('tm', 'rows')) / count  130 us
    unnamed x2, blocking collectives  127 us
    ppermute x9, starting transfers between devices, from_behind(): return lax.ppermute(array, axis, pairs)  115 us
    dot_general x9, matrix products, conv_taps(): jnp.dot(stacked.reshape(-1, 3 * chans), weight[step_t, step_h].reshape(3...  18.8 us
    unnamed x71, local copies, waits for them, and re-layouts  17.4 us
  transfers between devices with their start and end apart: 11, of which 7 were waited for; matrix products, arithmetic and copies ran while one was open for 4% of the time, Pallas kernels for 0%

profile of v1, /device:TPU:54, one launch (start us, length us, event | category | flops | bytes accessed | tf_op | source)
XLA Modules:
  0.0 681.6 jit_solution(11770985791621889881)
XLA Ops:
  1.7 63.7 %psum.14 = f32[32]{0:T(128)S(1)} all-reduce(f32[32]{0:T(128)S(1)} %reduce_sum.75), channel_id=1, replica_groups=mesh['tm'=2,'rows'=64] {'tm','rows'}, use_global_device_ids=true, to_apply=%region_2.0 | all-reduce | flops 32 | bytes 256 | tf_op jit(solution)/shard_map/psum | solution.py:40
  67.6 63.1 %all-reduce.1 = f32[4096]{0:T(1024)S(1)} all-reduce(f32[4096]{0:T(1024)S(1)} %dynamic-update-slice), channel_id=2, replica_groups=mesh['tm'=2,'rows'=64] {'tm','rows'}, use_global_device_ids=true, to_apply=%add.1 | all-reduce | flops 4096 | bytes 32768
  132.3 1.7 collective-permute-start
  134.1 2.1 collective-permute-done
  136.5 3.7 collective-permute-start.1
  140.1 2.4 collective-permute-start.2
  142.5 9.3 %fusion.44 = (bf16[1,1,3,512,512]{4,3,2,1,0:T(8,128)(2,1)S(1)}, bf16[1,1,3,512,512]{4,3,2,1,0:T(8,128)(2,1)}, bf16[1,1,3,512,512]{4,3,2,1,0:T(8,128)(2,1)}, bf16...) fusion(bf16[3,3,3,512,512]{4,3,2,1,0:T(8,128)(2,1)} %param.15), kind=kLoop, calls=%fused_computation.89 | loop fusion | bytes 28311552 | tf_op jit(solution)/shard_map/slice | solution.py:64
  151.8 10.6 %collective-permute-done.1 = bf16[4,1,240,512]{3,2,1,0:T(8,128)(2,1)S(1)} collective-permute-done((bf16[4,1,240,512]{3,2,1,0:T(8,128)(2,1)S(1)}, bf16[4,1,240,512]{3,2,1,0:T(8,128)(2,1)S(1)}, u32[]{:S(2)}, u32[]{:S(2)}) %collective-permute-start.1) | collective-permute-done | bytes 983072 | tf_op jit(solution)/shard_map/ppermute | solution.py:27
  162.4 4.4 collective-permute-done.2
  166.8 2.1 select_maximum_fusion
  168.9 4.5 fusion.45
  177.8 1.7 fusion.48
  179.5 1.7 fusion.50
  183.0 3.0 fusion.51
  186.0 1.7 fusion.53
  189.1 1.7 fusion.54
  191.7 3.2 fusion.49
  194.9 1.7 fusion.52
  196.6 1.7 fusion.55
  198.3 2.4 add_add_fusion
  201.4 66.4 %psum.15 = f32[32]{0:T(128)S(1)} all-reduce(f32[32]{0:T(128)S(1)} %reduce_sum.100), channel_id=1, replica_groups=mesh['tm'=2,'rows'=64] {'tm','rows'}, use_global_device_ids=true, to_apply=%region_8.9 | all-reduce | flops 32 | bytes 256 | tf_op jit(solution)/shard_map/psum | solution.py:40
  268.9 64.2 %all-reduce.2 = f32[4096]{0:T(1024)S(1)} all-reduce(f32[4096]{0:T(1024)S(1)} %dynamic-update-slice.1), channel_id=3, replica_groups=mesh['tm'=2,'rows'=64] {'tm','rows'}, use_global_device_ids=true, to_apply=%add.2 | all-reduce | flops 4096 | bytes 32768
  334.5 1.7 convolution_convert_fusion
  337.7 3.8 collective-permute-start.3
  341.5 3.3 collective-permute-start.4
  344.8 4.5 collective-permute-start.5
  349.3 3.0 collective-permute-start.6
  352.3 2.8 collective-permute-start.7
  355.1 30.5 %collective-permute-done.3 = bf16[2,2,2,240,512]{4,3,2,1,0:T(8,128)(2,1)} collective-permute-done((bf16[2,2,2,240,512]{4,3,2,1,0:T(8,128)(2,1)}, bf16[2,2,2,240,512]{4,3,2,1,0:T(8,128)(2,1)}, u32[]{:S(2)}, u32[]{:S(2)}) %collective-permute-start.3) | collective-permute-done | bytes 1966112 | tf_op jit(solution)/shard_map/ppermute | solution.py:16
  385.7 2.6 collective-permute-start.8
  388.3 39.4 %collective-permute-done.4 = bf16[2,2,2,240,512]{4,3,2,1,0:T(8,128)(2,1)} collective-permute-done((bf16[2,2,2,240,512]{4,3,2,1,0:T(8,128)(2,1)}, bf16[2,2,2,240,512]{4,3,2,1,0:T(8,128)(2,1)}, u32[]{:S(2)}, u32[]{:S(2)}) %collective-permute-start.4) | collective-permute-done | bytes 1966112 | tf_op jit(solution)/shard_map/ppermute | solution.py:16
  427.6 90.0 %collective-permute-start.9 = (bf16[2,2,2,240,512]{4,3,2,1,0:T(8,128)(2,1)}, bf16[2,2,2,240,512]{4,3,2,1,0:T(8,128)(2,1)}, u32[]{:S(2)}, u32[]{:S(2)}) collective-permute-start(bf16[2,2,2,240,512]{4,3,2,1,0:T(8,128)(2,1)} %pad_maximum_fusion.10), channel_id=1, source_target_pairs={{3,0},{4,1},{5,2},{6,3},{7,4},{8,5},{9,6},{10,7},{11,8},{12,9},{13... | collective-permute-start | bytes 5898248 | tf_op jit(solution)/shard_map/ppermute | solution.py:16
  517.7 3.1 collective-permute-start.10
  521.0 2.8 convolution_convert_fusion.2
  523.8 1.7 constant_dynamic-update-slice_fusion.8
  525.4 1.7 constant_dynamic-update-slice_fusion.7
  527.1 1.7 constant_dynamic-update-slice_fusion.6
  528.8 1.7 constant_dynamic-update-slice_fusion.5
  530.6 1.7 constant_dynamic-update-slice_fusion.3
  532.3 1.7 constant_dynamic-update-slice_fusion.2
  534.0 27.2 %collective-permute-done.9 = bf16[2,2,2,240,512]{4,3,2,1,0:T(8,128)(2,1)} collective-permute-done((bf16[2,2,2,240,512]{4,3,2,1,0:T(8,128)(2,1)}, bf16[2,2,2,240,512]{4,3,2,1,0:T(8,128)(2,1)}, u32[]{:S(2)}, u32[]{:S(2)}) %collective-permute-start.9) | collective-permute-done | bytes 1966112 | tf_op jit(solution)/shard_map/ppermute | solution.py:16
  561.2 1.7 constant_dynamic-update-slice_fusion.1
  562.9 80.4 %collective-permute-done.10 = bf16[2,2,2,240,512]{4,3,2,1,0:T(8,128)(2,1)} collective-permute-done((bf16[2,2,2,240,512]{4,3,2,1,0:T(8,128)(2,1)}, bf16[2,2,2,240,512]{4,3,2,1,0:T(8,128)(2,1)}, u32[]{:S(2)}, u32[]{:S(2)}) %collective-permute-start.10) | collective-permute-done | bytes 1966112 | tf_op jit(solution)/shard_map/ppermute | solution.py:16
  643.3 1.7 constant_dynamic-update-slice_fusion
  645.0 4.3 fusion.43
  649.3 10.1 %fusion = (f32[2,480]{1,0:T(2,128)S(1)}, f32[2,480,4320]{2,1,0:T(8,128)}) fusion(pred[4320]{0:T(1024)(128)(4,1)S(1)} %broadcast_in_dim.35, bf16[2,480,512]{2,1,0:T(8,128)(2,1)} %bitcast.89, bf16[2,4320,512]{2,1,0:T(8,128)(2,1)S(1)} %bitcast.63), kind=kOutput, calls=%fused_computation.2 | convolution fusion | flops 4259173376 | bytes 26427360 | tf_op jit(solution)/shard_map/fqc,fkc->fqk/dot_general | solution.py:124
  659.4 9.5 %fusion.1 = f32[2,480]{1,0:T(2,128)S(1)} fusion(f32[2,480,4320]{2,1,0:T(8,128)} %get-tuple-element.50, f32[2,480]{1,0:T(2,128)S(1)} %get-tuple-element.49, pred[4320]{0:T(1024)(128)(4,1)S(1)} %broadcast_in_dim.35), kind=kLoop, calls=%fused_computation.3 | loop fusion | flops 16587840 | bytes 16600800 | tf_op jit(solution)/shard_map/reduce_sum | solution.py:128
  668.9 11.0 %divide_convert_fusion = bf16[2,480,512]{2,1,0:T(8,128)(2,1)S(1)} fusion(bf16[2,4320,512]{2,1,0:T(8,128)(2,1)} %bitcast.62, f32[2,480,4320]{2,1,0:T(8,128)} %get-tuple-element.50, f32[2,480]{1,0:T(2,128)S(1)} %get-tuple-element.49, pred[4320]{0:T(1024)(128)(4,1)S(1)} %broadcast_in_dim.35, f32[2,480]{1,0:T(2,128)S(1)} %fusion.1), kind=kOutput, calls=%fused_computation.62 | convolution fusion | flops 4264304640 | bytes 26431200 | tf_op jit(solution)/shard_map/fqk,fkc->fqc/dot_general | solution.py:129
  (115 shorter events, 20.6 us)
Async XLA Ops:
  0.0 333.8 %copy-start = (bf16[512,512]{1,0:T(8,128)(2,1)S(1)}, bf16[512,512]{1,0:T(8,128)(2,1)}, u32[]{:S(2)}) copy-start(bf16[512,512]{1,0:T(8,128)(2,1)} %param.20) | copy-start | bytes 1572868
  0.0 130.9 %copy-start.2 = (bf16[2,2,240,512]{3,2,1,0:T(8,128)(2,1)S(1)}, bf16[2,2,240,512]{3,2,1,0:T(8,128)(2,1)}, u32[]{:S(2)}) copy-start(bf16[2,2,240,512]{3,2,1,0:T(8,128)(2,1)} %param.12) | copy-start | bytes 2949124
  132.3 3.9 collective-permute-start
  136.5 25.9 %collective-permute-start.1 = (bf16[4,1,240,512]{3,2,1,0:T(8,128)(2,1)S(1)}, bf16[4,1,240,512]{3,2,1,0:T(8,128)(2,1)S(1)}, u32[]{:S(2)}, u32[]{:S(2)}) collective-permute-start(bf16[4,1,240,512]{3,2,1,0:T(8,128)(2,1)S(1)} %get-tuple-element.44), channel_id=1, source_target_pairs={{0,1},{1,2},{2,3},{3,4},{4,5},{5,6},{6,7},{7,8},{8,9},{9,10},{10,1... | collective-permute-start | bytes 2949128 | tf_op jit(solution)/shard_map/ppermute | solution.py:27
  140.1 26.7 %collective-permute-start.2 = (bf16[4,1,240,512]{3,2,1,0:T(8,128)(2,1)S(1)}, bf16[4,1,240,512]{3,2,1,0:T(8,128)(2,1)S(1)}, u32[]{:S(2)}, u32[]{:S(2)}) collective-permute-start(bf16[4,1,240,512]{3,2,1,0:T(8,128)(2,1)S(1)} %get-tuple-element.45), channel_id=1, source_target_pairs={{1,0},{2,1},{3,2},{4,3},{5,4},{6,5},{7,6},{8,7},{9,8},{10,9},{11,1... | collective-permute-start | bytes 2949128 | tf_op jit(solution)/shard_map/ppermute | solution.py:29
  174.3 1.2 copy-start.11
  174.3 1.5 copy-start.12
  174.3 1.8 copy-start.13
  174.3 2.1 copy-start.14
  176.4 1.4 copy-start.22
  177.8 1.7 copy-start.21
  179.5 1.7 copy-start.7
  179.5 1.7 copy-start.8
  179.5 1.8 copy-start.9
  179.5 2.1 copy-start.10
  181.6 1.4 copy-start.20
  183.0 3.0 copy-start.19
  186.0 1.7 copy-start.5
  186.0 1.7 copy-start.6
  187.7 1.4 copy-start.18
  191.7 3.2 copy-start.17
  194.9 1.7 copy-start.16
  196.6 1.7 copy-start.15
  198.3 2.5 copy-start.25
  200.8 132.6 %copy-start.26 = (f32[512]{0:T(512)S(1)}, f32[512]{0:T(512)}, u32[]{:S(2)}) copy-start(f32[512]{0:T(512)} %param.18) | copy-start | bytes 6148
  200.8 132.6 %copy-start.27 = (f32[512]{0:T(512)S(1)}, f32[512]{0:T(512)}, u32[]{:S(2)}) copy-start(f32[512]{0:T(512)} %param.17) | copy-start | bytes 6148
  201.2 133.2 %copy-start.3 = (bf16[2,2,240,512]{3,2,1,0:T(8,128)(2,1)}, bf16[2,2,240,512]{3,2,1,0:T(8,128)(2,1)S(1)}, u32[]{:S(2)}) copy-start(bf16[2,2,240,512]{3,2,1,0:T(8,128)(2,1)S(1)} %get-tuple-element.6) | copy-start | bytes 2949124
  333.8 2.4 copy-start.23
  336.2 184.8 %copy-start.24 = (bf16[2,2,240,512]{3,2,1,0:T(8,128)(2,1)S(1)}, bf16[2,2,240,512]{3,2,1,0:T(8,128)(2,1)}, u32[]{:S(2)}) copy-start(bf16[2,2,240,512]{3,2,1,0:T(8,128)(2,1)} %copy-done.23) | copy-start | bytes 2949124
  337.7 48.0 %collective-permute-start.3 = (bf16[2,2,2,240,512]{4,3,2,1,0:T(8,128)(2,1)}, bf16[2,2,2,240,512]{4,3,2,1,0:T(8,128)(2,1)}, u32[]{:S(2)}, u32[]{:S(2)}) collective-permute-start(bf16[2,2,2,240,512]{4,3,2,1,0:T(8,128)(2,1)} %pad_maximum_fusion.10), channel_id=1, source_target_pairs={{0,4},{1,5},{2,6},{3,7},{4,8},{5,9},{6,10},{7,11},{8,12},{9,13},{1... | collective-permute-start | bytes 5898248 | tf_op jit(solution)/shard_map/ppermute | solution.py:16
  341.5 86.1 %collective-permute-start.4 = (bf16[2,2,2,240,512]{4,3,2,1,0:T(8,128)(2,1)}, bf16[2,2,2,240,512]{4,3,2,1,0:T(8,128)(2,1)}, u32[]{:S(2)}, u32[]{:S(2)}) collective-permute-start(bf16[2,2,2,240,512]{4,3,2,1,0:T(8,128)(2,1)} %pad_maximum_fusion.10), channel_id=1, source_target_pairs={{0,3},{1,4},{2,5},{3,6},{4,7},{5,8},{6,9},{7,10},{8,11},{9,12},{10... | collective-permute-start | bytes 5898248 | tf_op jit(solution)/shard_map/ppermute | solution.py:16
  344.8 172.9 %collective-permute-start.5 = (bf16[2,2,2,240,512]{4,3,2,1,0:T(8,128)(2,1)}, bf16[2,2,2,240,512]{4,3,2,1,0:T(8,128)(2,1)}, u32[]{:S(2)}, u32[]{:S(2)}) collective-permute-start(bf16[2,2,2,240,512]{4,3,2,1,0:T(8,128)(2,1)} %pad_maximum_fusion.10), channel_id=1, source_target_pairs={{0,2},{1,3},{2,4},{3,5},{4,6},{5,7},{6,8},{7,9},{8,10},{9,11},{10,... | collective-permute-start | bytes 5898248 | tf_op jit(solution)/shard_map/ppermute | solution.py:16
  349.3 179.5 %collective-permute-start.6 = (bf16[2,2,2,240,512]{4,3,2,1,0:T(8,128)(2,1)}, bf16[2,2,2,240,512]{4,3,2,1,0:T(8,128)(2,1)}, u32[]{:S(2)}, u32[]{:S(2)}) collective-permute-start(bf16[2,2,2,240,512]{4,3,2,1,0:T(8,128)(2,1)} %pad_maximum_fusion.10), channel_id=1, source_target_pairs={{0,1},{1,2},{2,3},{3,4},{4,5},{5,6},{6,7},{7,8},{8,9},{9,10},{10,1... | collective-permute-start | bytes 5898248 | tf_op jit(solution)/shard_map/ppermute | solution.py:16
  352.3 178.3 %collective-permute-start.7 = (bf16[2,2,2,240,512]{4,3,2,1,0:T(8,128)(2,1)}, bf16[2,2,2,240,512]{4,3,2,1,0:T(8,128)(2,1)}, u32[]{:S(2)}, u32[]{:S(2)}) collective-permute-start(bf16[2,2,2,240,512]{4,3,2,1,0:T(8,128)(2,1)} %pad_maximum_fusion.10), channel_id=1, source_target_pairs={{1,0},{2,1},{3,2},{4,3},{5,4},{6,5},{7,6},{8,7},{9,8},{10,9},{11,1... | collective-permute-start | bytes 5898248 | tf_op jit(solution)/shard_map/ppermute | solution.py:16
  385.7 146.6 %collective-permute-start.8 = (bf16[2,2,2,240,512]{4,3,2,1,0:T(8,128)(2,1)}, bf16[2,2,2,240,512]{4,3,2,1,0:T(8,128)(2,1)}, u32[]{:S(2)}, u32[]{:S(2)}) collective-permute-start(bf16[2,2,2,240,512]{4,3,2,1,0:T(8,128)(2,1)} %pad_maximum_fusion.10), channel_id=1, source_target_pairs={{2,0},{3,1},{4,2},{5,3},{6,4},{7,5},{8,6},{9,7},{10,8},{11,9},{12,... | collective-permute-start | bytes 5898248 | tf_op jit(solution)/shard_map/ppermute | solution.py:16
  427.6 133.6 %collective-permute-start.9 = (bf16[2,2,2,240,512]{4,3,2,1,0:T(8,128)(2,1)}, bf16[2,2,2,240,512]{4,3,2,1,0:T(8,128)(2,1)}, u32[]{:S(2)}, u32[]{:S(2)}) collective-permute-start(bf16[2,2,2,240,512]{4,3,2,1,0:T(8,128)(2,1)} %pad_maximum_fusion.10), channel_id=1, source_target_pairs={{3,0},{4,1},{5,2},{6,3},{7,4},{8,5},{9,6},{10,7},{11,8},{12,9},{13... | collective-permute-start | bytes 5898248 | tf_op jit(solution)/shard_map/ppermute | solution.py:16
  517.7 125.6 %collective-permute-start.10 = (bf16[2,2,2,240,512]{4,3,2,1,0:T(8,128)(2,1)}, bf16[2,2,2,240,512]{4,3,2,1,0:T(8,128)(2,1)}, u32[]{:S(2)}, u32[]{:S(2)}) collective-permute-start(bf16[2,2,2,240,512]{4,3,2,1,0:T(8,128)(2,1)} %pad_maximum_fusion.10), channel_id=1, source_target_pairs={{4,0},{5,1},{6,2},{7,3},{8,4},{9,5},{10,6},{11,7},{12,8},{13,9},{1... | collective-permute-start | bytes 5898248 | tf_op jit(solution)/shard_map/ppermute | solution.py:16
  668.9 11.1 %copy-start.4 = (bf16[2,2,240,512]{3,2,1,0:T(8,128)(2,1)S(1)}, bf16[2,2,240,512]{3,2,1,0:T(8,128)(2,1)}, u32[]{:S(2)}) copy-start(bf16[2,2,240,512]{3,2,1,0:T(8,128)(2,1)} %copy-done.3) | copy-start | bytes 2949124
  668.9 11.1 %copy-start.28 = (bf16[512,512]{1,0:T(8,128)(2,1)S(1)}, bf16[512,512]{1,0:T(8,128)(2,1)}, u32[]{:S(2)}) copy-start(bf16[512,512]{1,0:T(8,128)(2,1)} %param.22) | copy-start | bytes 1572868
  668.9 11.1 %copy-start.29 = (f32[512]{0:T(512)S(1)}, f32[512]{0:T(512)}, u32[]{:S(2)}) copy-start(f32[512]{0:T(512)} %param.23) | copy-start | bytes 6148
  668.9 12.7 %copy-start.1 = (bf16[512,512]{1,0:T(8,128)(2,1)S(1)}, bf16[512,512]{1,0:T(8,128)(2,1)}, u32[]{:S(2)}) copy-start(bf16[512,512]{1,0:T(8,128)(2,1)} %param.20) | copy-start | bytes 1572868
